TPU v7x, 256 devices: a whole 4x4x8 slice. The times are simulated.
256 devices in a mesh: dp: 32 (over z, y_hi, core), expert: 8 (over x, y_lo).
Axes of the slice: x: 4, y: 4 (y_hi: 2, y_lo: 2; y = y_hi * 2 + y_lo), z: 8, core: 2. Of those that a mesh axis runs over, the one named last changes fastest.
Arguments:
- tokens: bfloat16 [32768, 2048], P(('dp', 'expert')), may hold values from -24 to 24
- cotangent: bfloat16 [32768, 2048], P(('dp', 'expert')), may hold values from -24 to 24
- expert_ids: int32 [32768, 2], P(('dp', 'expert')), may hold values from 0 to 7, all different within a row; in each aligned block of 128 rows (0 to 127, 128 to 255, ...) at most 40 rows name the same one
- gate_weights: float32 [32768, 2], P(('dp', 'expert')), may hold values from 0.1 to 1
- partner: int32 [8], replicated, may hold values from 0 to 7, as said below
- w_gate: bfloat16 [8, 2048, 768], P('expert'), may hold values from -0.125 to 0.125
- w_up: bfloat16 [8, 2048, 768], P('expert'), may hold values from -0.125 to 0.125
- w_down: bfloat16 [8, 768, 2048], P('expert'), may hold values from -0.21875 to 0.21875
Outputs:
- mixed_out: bfloat16 [32768, 2048], P(('dp', 'expert'))
- token_grad: bfloat16 [32768, 2048], P(('dp', 'expert'))
- gate_grad: float32 [32768, 2], P(('dp', 'expert'))
- slot_grad_gate: float32 [8, 2048, 768], P('expert', 'dp')
- slot_grad_up: float32 [8, 2048, 768], P('expert', 'dp')
- slot_grad_down: float32 [8, 768, 2048], P('expert', None, 'dp')
Inputs may be any that keep to these rules, and one draw needn't show every extreme that they name: `expert_ids`: each row names 2 different experts. Among the 128 rows of one device no expert is named by more than 40 rows, and in every draw some device names some expert exactly 40 times. partner[partner[i]] = i and partner[i] != i for every slot i.
All inputs are finite; a program needn't handle non-finite values.
Results may differ from a plain program's by a relative error of at most 0.015.
Values may be sent and summed in bfloat16 or wider, within the bound.
A program may use at most 128 MiB of HBM per device.

v0:
```python
import jax
import jax.numpy as jnp
from jax import lax
from jax.sharding import PartitionSpec as P


def as_sent(shard):

    def short(part):
        return part.astype(jnp.bfloat16) if part.dtype == jnp.float32 else part

    return jax.tree.map(short, shard)


def contract_rows(left_mat, right_mat):
    return lax.dot_general(
        left_mat, right_mat, (((0,), (0,)), ((), ())), preferred_element_type=jnp.float32
    )


def contract_cols(left_mat, right_mat):
    return lax.dot_general(
        left_mat, right_mat, (((1,), (1,)), ((), ())), preferred_element_type=jnp.float32
    )


def pick_from(stacked, source):
    return lax.dynamic_index_in_dim(stacked, source, 0, keepdims=False)


def shards(tokens, cotangent, expert_ids, gate_weights, partner, w_gate, w_up, w_down):
    groups = lax.axis_size("expert")
    my_group = lax.axis_index("expert")
    tok_count, model_width = tokens.shape
    top_count = expert_ids.shape[1]
    capacity = min(tok_count, 5 * tok_count * top_count // (4 * groups))
    buffer_rows = groups * capacity
    group_ids = jnp.arange(groups, dtype=jnp.int32)
    my_mate = pick_from(partner, my_group)
    flat_ids = expert_ids.reshape(-1)
    dest_group = jnp.sum(
        jnp.where(flat_ids[:, None] == group_ids[None, :], partner[None, :], 0), axis=1
    )
    one_hot = (dest_group[:, None] == group_ids[None, :]).astype(jnp.int32)
    earlier = jnp.cumsum(one_hot, axis=0) - one_hot
    slot_index = dest_group * capacity + jnp.sum(earlier * one_hot, axis=1)
    place_mat = (slot_index[None, :] == jnp.arange(buffer_rows, dtype=jnp.int32)[:, None]).astype(
        jnp.bfloat16
    )
    replicas = lax.axis_size("dp")
    share_rows = model_width // replicas
    share_start = lax.axis_index("dp") * share_rows
    shares = (
        lax.dynamic_slice_in_dim(w_gate[0], share_start, share_rows, 0),
        lax.dynamic_slice_in_dim(w_up[0], share_start, share_rows, 0),
        lax.dynamic_slice_in_dim(w_down[0], share_start, share_rows, 1),
    )
    is_mate = (partner == my_group)[:, None, None]
    outgoing = tuple(
        (
            jnp.where(is_mate, own_share[None], jnp.zeros_like(own_share)[None])
            for own_share in shares
        )
    )
    incoming = jax.tree.map(
        lambda part, own: part.astype(own.dtype),
        lax.all_to_all(as_sent(outgoing), "expert", split_axis=0, concat_axis=0, tiled=True),
        outgoing,
    )
    mate_shares = tuple((pick_from(block_piece, my_mate) for block_piece in incoming))
    gate_mat, up_mat, down_mat = (
        lax.all_gather(mate_shares[0], "dp", axis=0, tiled=True),
        lax.all_gather(mate_shares[1], "dp", axis=0, tiled=True),
        lax.all_gather(mate_shares[2], "dp", axis=1, tiled=True),
    )
    repeated = jnp.repeat(tokens, top_count, axis=0)
    outgoing_rows = jnp.dot(place_mat, repeated, preferred_element_type=jnp.float32).astype(
        jnp.bfloat16
    )
    expert_in = lax.all_to_all(
        outgoing_rows.reshape(groups, capacity, model_width),
        "expert",
        split_axis=0,
        concat_axis=0,
        tiled=True,
    ).reshape(buffer_rows, model_width)
    gate_pre = jnp.dot(expert_in, gate_mat, preferred_element_type=jnp.float32)
    up_pre = jnp.dot(expert_in, up_mat, preferred_element_type=jnp.float32)
    sigmoid_gate = jax.nn.sigmoid(gate_pre)
    hidden = (gate_pre * sigmoid_gate * up_pre).astype(jnp.bfloat16)
    expert_out = jnp.dot(hidden, down_mat, preferred_element_type=jnp.float32).astype(jnp.bfloat16)
    returned = lax.all_to_all(
        expert_out.reshape(groups, capacity, model_width),
        "expert",
        split_axis=0,
        concat_axis=0,
        tiled=True,
    ).reshape(buffer_rows, model_width)
    per_assign = (
        jnp.take(returned, slot_index, axis=0)
        .astype(jnp.float32)
        .reshape(tok_count, top_count, model_width)
    )
    mixed_out = jnp.sum(gate_weights[:, :, None] * per_assign, axis=1).astype(jnp.bfloat16)
    cot_float = cotangent.astype(jnp.float32)
    gate_grad = jnp.sum(cot_float[:, None, :] * per_assign, axis=2)
    scaled = (
        (gate_weights[:, :, None] * cot_float[:, None, :])
        .astype(jnp.bfloat16)
        .reshape(-1, model_width)
    )
    outgoing_grads = jnp.dot(place_mat, scaled, preferred_element_type=jnp.float32).astype(
        jnp.bfloat16
    )
    grads_in = lax.all_to_all(
        outgoing_grads.reshape(groups, capacity, model_width),
        "expert",
        split_axis=0,
        concat_axis=0,
        tiled=True,
    ).reshape(buffer_rows, model_width)
    hidden_grad = contract_cols(grads_in, down_mat)
    gate_grad_pre = (
        hidden_grad * up_pre * sigmoid_gate * (1.0 + gate_pre * (1.0 - sigmoid_gate))
    ).astype(jnp.bfloat16)
    up_grad_pre = (hidden_grad * gate_pre * sigmoid_gate).astype(jnp.bfloat16)
    row_grad = (contract_cols(gate_grad_pre, gate_mat) + contract_cols(up_grad_pre, up_mat)).astype(
        jnp.bfloat16
    )
    returned_grads = lax.all_to_all(
        row_grad.reshape(groups, capacity, model_width),
        "expert",
        split_axis=0,
        concat_axis=0,
        tiled=True,
    ).reshape(buffer_rows, model_width)
    grad_rows = (
        jnp.take(returned_grads, slot_index, axis=0)
        .astype(jnp.float32)
        .reshape(tok_count, top_count, model_width)
    )
    token_grad = jnp.sum(grad_rows, axis=1).astype(jnp.bfloat16)
    partial_gate = contract_rows(expert_in, gate_grad_pre)
    partial_up = contract_rows(expert_in, up_grad_pre)
    partial_down = contract_rows(hidden, grads_in)
    sum_gate, sum_up, sum_down = (
        lax.psum_scatter(
            partial_gate.astype(jnp.bfloat16), "dp", scatter_dimension=0, tiled=True
        ).astype(jnp.float32),
        lax.psum_scatter(
            partial_up.astype(jnp.bfloat16), "dp", scatter_dimension=0, tiled=True
        ).astype(jnp.float32),
        lax.psum_scatter(
            partial_down.astype(jnp.bfloat16), "dp", scatter_dimension=1, tiled=True
        ).astype(jnp.float32),
    )
    return (mixed_out, token_grad, gate_grad, sum_gate[None], sum_up[None], sum_down[None])


def solution(mesh):
    in_specs = (
        P(("dp", "expert"), None),
        P(("dp", "expert"), None),
        P(("dp", "expert"), None),
        P(("dp", "expert"), None),
        P(),
        P("expert", None, None),
        P("expert", None, None),
        P("expert", None, None),
    )
    out_specs = (
        P(("dp", "expert"), None),
        P(("dp", "expert"), None),
        P(("dp", "expert"), None),
        P("expert", "dp", None),
        P("expert", "dp", None),
        P("expert", None, "dp"),
    )
    return jax.shard_map(shards, mesh=mesh, in_specs=in_specs, out_specs=out_specs, check_vma=False)
```

profile of v0, /device:TPU:4, one launch (start us, length us, event | category | flops | bytes accessed | tf_op | source)
XLA Modules:
  0.0 688.2 jit_solution(8233593337685913203)
XLA Ops:
  7.2 0.8 broadcast_compare_fusion
  8.0 1.1 dynamic-slice_bitcast_fusion
  9.1 1.3 broadcast_select_fusion.3
  10.5 6.3 all-to-all-start.2
  16.8 0.6 dynamic_slice.25
  19.3 7.3 %all-to-all-done.2 = bf16[8,64,768]{2,1,0:T(8,128)(2,1)} async-done(((bf16[8,64,768]{2,1,0:T(8,128)(2,1)}), bf16[8,64,768]{2,1,0:T(8,128)(2,1)}, u32[]{:S(2)}, u32[]{:S(2)}) %all-to-all-start.2) | async-done | bytes 786464 | tf_op jit(solution)/shard_map/all_to_all | solution.py:67
  26.6 1.5 constant_dynamic-slice_fusion.2
  28.2 0.1 constant_dynamic-slice_fusion.1
  28.4 0.1 copy.28
  28.5 0.1 broadcast_select_fusion.1
  28.7 15.4 %all_to_all.35 = bf16[8,768,64]{1,2,0:T(8,128)(2,1)S(1)} all-to-all(bf16[8,768,64]{1,2,0:T(8,128)(2,1)S(1)} %broadcast_select_fusion.1), channel_id=1, replica_groups=mesh['dp'=32,'expert'=8] {'expert'}, dimensions={0} | all-to-all | bytes 1572864 | tf_op jit(solution)/shard_map/all_to_all | solution.py:67
  44.0 0.6 constant_dynamic-slice_fusion
  44.8 13.8 %all_to_all.36 = bf16[8,64,768]{2,1,0:T(8,128)(2,1)S(1)} all-to-all(bf16[8,64,768]{2,1,0:T(8,128)(2,1)S(1)} %copy-done.6), channel_id=1, replica_groups=mesh['dp'=32,'expert'=8] {'expert'}, dimensions={0} | all-to-all | bytes 1572864 | tf_op jit(solution)/shard_map/all_to_all | solution.py:67
  58.6 0.6 constant_dynamic-slice_fusion.3
  59.3 0.1 copy.24
  59.4 0.1 eq.57
  59.5 0.1 select_reduce_fusion
  59.6 0.6 reduce-window.6
  60.2 0.2 slice_reduce_fusion
  60.5 0.6 broadcast_in_dim.123
  61.1 0.4 reshape.92
  61.7 1.6 convolution_convert_fusion.4
  63.2 6.2 all-to-all-start
  69.5 2.4 mul.83
  71.9 2.7 mul.84
  74.6 0.1 copy.23
  74.7 0.1 mul.81
  74.9 1.7 convolution_convert_fusion.3
  76.5 6.3 all-to-all-done
  82.8 7.1 %all-to-all-start.5 = ((bf16[8,40,2048]{2,1,0:T(8,128)(2,1)}), bf16[8,40,2048]{2,1,0:T(8,128)(2,1)}, u32[]{:S(2)}, u32[]{:S(2)}) async-start(bf16[8,40,2048]{2,1,0:T(8,128)(2,1)} %bitcast.70), calls=%async_computation.5 | async-start | bytes 2621440 | tf_op jit(solution)/shard_map/all_to_all | solution.py:115
  89.9 34.6 %all-gather.9.cloned.1.call-done = bf16[1,2048,768]{2,1,0:T(8,128)(2,1)} async-done(((bf16[1,64,768]{2,1,0:T(8,128)(2,1)}), bf16[1,2048,768]{2,1,0:T(8,128)(2,1)}) %all-gather.9.cloned.1.call-update) | async-done | bytes 3145744 | tf_op jit(solution)/shard_map/all_gather | solution.py:73
  124.5 3.5 fusion.6
  128.0 79.0 %all-gather.11.cloned.1.call-done = bf16[1,768,2048]{1,2,0:T(8,128)(2,1)} async-done(((bf16[1,768,64]{1,2,0:T(8,128)(2,1)}), bf16[1,768,2048]{1,2,0:T(8,128)(2,1)}) %all-gather.11.cloned.1.call-update) | async-done | bytes 3145744 | tf_op jit(solution)/shard_map/all_gather | solution.py:74
  206.9 3.5 fusion
  210.4 79.6 %all-gather.7.cloned.1.call-done = bf16[1,2048,768]{2,1,0:T(8,128)(2,1)} async-done(((bf16[1,64,768]{2,1,0:T(8,128)(2,1)}), bf16[1,2048,768]{2,1,0:T(8,128)(2,1)}) %all-gather.7.cloned.1.call-update) | async-done | bytes 3145744 | tf_op jit(solution)/shard_map/all_gather | solution.py:72
  290.0 3.7 multiply_convert_fusion.3
  293.8 0.8 copy-done.15
  294.5 4.8 convolution_convert_fusion
  299.4 0.2 reduce-scatter.6.cloned.1.call-start
  299.6 4.9 convolution_convert_fusion.1
  304.5 4.8 convolution_convert_fusion.2
  309.4 3.3 fusion.4
  312.8 2.3 fusion.15
  315.1 5.0 all-to-all-start.6
  320.0 4.3 fusion.18
  324.3 12.7 %all-to-all-done.6 = bf16[8,40,2048]{2,1,0:T(8,128)(2,1)S(1)} async-done(((bf16[8,40,2048]{2,1,0:T(8,128)(2,1)}), bf16[8,40,2048]{2,1,0:T(8,128)(2,1)S(1)}, u32[]{:S(2)}, u32[]{:S(2)}) %all-to-all-start.6) | async-done | bytes 1310752 | tf_op jit(solution)/shard_map/all_to_all | solution.py:130
  337.0 7.2 %all-to-all-start.4 = ((bf16[8,40,2048]{2,1,0:T(8,128)(2,1)}), bf16[8,40,2048]{2,1,0:T(8,128)(2,1)S(1)}, u32[]{:S(2)}, u32[]{:S(2)}) async-start(bf16[8,40,2048]{2,1,0:T(8,128)(2,1)} %bitcast.71), calls=%async_computation.4 | async-start | bytes 2621440 | tf_op jit(solution)/shard_map/all_to_all | solution.py:92
  344.2 2.3 gather_fusion.1
  346.5 15.8 %all-to-all-done.4 = bf16[8,40,2048]{2,1,0:T(8,128)(2,1)S(1)} async-done(((bf16[8,40,2048]{2,1,0:T(8,128)(2,1)}), bf16[8,40,2048]{2,1,0:T(8,128)(2,1)S(1)}, u32[]{:S(2)}, u32[]{:S(2)}) %all-to-all-start.4) | async-done | bytes 1310752 | tf_op jit(solution)/shard_map/all_to_all | solution.py:92
  362.4 1.4 gather_fusion
  363.7 2.9 broadcast_select_fusion
  366.6 2.2 reshape.97
  368.8 2.7 reshape.102
  371.5 0.4 multiply_reduce_fusion
  372.0 0.1 reduce_sum.52
  372.1 0.6 copy.27
  372.7 4.7 reduce.1
  377.5 5.6 multiply_reduce_fusion.1
  383.1 45.0 %reduce-scatter.8.cloned.1.call-done = bf16[768,64]{0,1:T(8,128)(2,1)} async-done(((bf16[768,2048]{0,1:T(8,128)(2,1)}), bf16[768,64]{0,1:T(8,128)(2,1)}) %reduce-scatter.8.cloned.1.call-update) | async-done | bytes 98320 | tf_op jit(solution)/shard_map/reduce_scatter | solution.py:153
  428.1 1.6 bitcast_convert_fusion
  429.7 124.2 %reduce-scatter.6.cloned.1.call-done = bf16[64,768]{1,0:T(8,128)(2,1)} async-done(((bf16[2048,768]{1,0:T(8,128)(2,1)}), bf16[64,768]{1,0:T(8,128)(2,1)}) %reduce-scatter.6.cloned.1.call-update) | async-done | bytes 98320 | tf_op jit(solution)/shard_map/reduce_scatter | solution.py:150
  553.9 1.6 bitcast_convert_fusion.1
  555.5 124.2 %reduce-scatter.4.cloned.1.call-done = bf16[64,768]{1,0:T(8,128)(2,1)} async-done(((bf16[2048,768]{1,0:T(8,128)(2,1)}), bf16[64,768]{1,0:T(8,128)(2,1)}) %reduce-scatter.4.cloned.1.call-update) | async-done | bytes 98320 | tf_op jit(solution)/shard_map/reduce_scatter | solution.py:147
  679.8 1.6 bitcast_convert_fusion.2
  (52 shorter events, 0.5 us)
Async XLA Ops:
  7.2 21.0 %copy-start = (bf16[1,768,2048]{2,1,0:T(8,128)(2,1)S(1)}, bf16[1,768,2048]{2,1,0:T(8,128)(2,1)}, u32[]{:S(2)}) copy-start(bf16[1,768,2048]{2,1,0:T(8,128)(2,1)} %param.17) | copy-start | bytes 9437188
  7.2 9.6 %copy-start.11 = (s32[8]{0:T(128)S(1)}, s32[8]{0:T(128)}, u32[]{:S(2)}) copy-start(s32[8]{0:T(128)} %param.14) | copy-start | bytes 100
  10.5 16.1 %all-to-all-start.2 = ((bf16[8,64,768]{2,1,0:T(8,128)(2,1)}), bf16[8,64,768]{2,1,0:T(8,128)(2,1)}, u32[]{:S(2)}, u32[]{:S(2)}) async-start(bf16[8,64,768]{2,1,0:T(8,128)(2,1)} %get-tuple-element.33), calls=%async_computation.2 | async-start | bytes 1572864 | tf_op jit(solution)/shard_map/all_to_all | solution.py:67
  16.8 107.7 %all-gather.9.cloned.1.call-start = ((), (), s32[]{:S(2)}) async-start(), calls=%async_computation.14 | async-start | bytes 3244032 | tf_op jit(solution)/shard_map/all_gather | solution.py:73
  28.2 178.8 %all-gather.11.cloned.1.call-start = ((), (), s32[]{:S(2)}) async-start(), calls=%async_computation.15 | async-start | bytes 3244032 | tf_op jit(solution)/shard_map/all_gather | solution.py:74
  28.4 16.4 %copy-start.6 = (bf16[8,64,768]{2,1,0:T(8,128)(2,1)S(1)}, bf16[8,64,768]{2,1,0:T(8,128)(2,1)}, u32[]{:S(2)}) copy-start(bf16[8,64,768]{2,1,0:T(8,128)(2,1)} %get-tuple-element.32) | copy-start | bytes 2359300
  28.5 30.8 %copy-start.9 = (s32[128,2]{0,1:T(2,128)S(1)}, s32[128,2]{0,1:T(2,128)}, u32[]{:S(2)}) copy-start(s32[128,2]{0,1:T(2,128)} %param.12) | copy-start | bytes 3076
  28.6 31.8 %copy-start.7 = (bf16[128,2048]{1,0:T(8,128)(2,1)S(1)}, bf16[128,2048]{1,0:T(8,128)(2,1)}, u32[]{:S(2)}) copy-start(bf16[128,2048]{1,0:T(8,128)(2,1)} %param.10) | copy-start | bytes 1572868
  44.7 245.3 %all-gather.7.cloned.1.call-start = ((), (), s32[]{:S(2)}) async-start(), calls=%async_computation.13 | async-start | bytes 3244032 | tf_op jit(solution)/shard_map/all_gather | solution.py:72
  61.7 7.8 %copy-start.8 = (bf16[128,2048]{1,0:T(8,128)(2,1)S(1)}, bf16[128,2048]{1,0:T(8,128)(2,1)}, u32[]{:S(2)}) copy-start(bf16[128,2048]{1,0:T(8,128)(2,1)} %param.11) | copy-start | bytes 1572868
  63.2 19.6 %all-to-all-start = ((bf16[8,40,2048]{2,1,0:T(8,128)(2,1)}), bf16[8,40,2048]{2,1,0:T(8,128)(2,1)}, u32[]{:S(2)}, u32[]{:S(2)}) async-start(bf16[8,40,2048]{2,1,0:T(8,128)(2,1)} %bitcast.3), calls=%async_computation | async-start | bytes 2621440 | tf_op jit(solution)/shard_map/all_to_all | solution.py:80
  71.9 2.7 copy-start.10
  74.6 8.2 %copy-start.2 = (f32[256,2048]{1,0:T(8,128)}, f32[256,2048]{1,0:T(8,128)S(1)}, u32[]{:S(2)}) copy-start(f32[256,2048]{1,0:T(8,128)S(1)} %mul.84) | copy-start | bytes 6291460
  82.8 45.1 %all-to-all-start.5 = ((bf16[8,40,2048]{2,1,0:T(8,128)(2,1)}), bf16[8,40,2048]{2,1,0:T(8,128)(2,1)}, u32[]{:S(2)}, u32[]{:S(2)}) async-start(bf16[8,40,2048]{2,1,0:T(8,128)(2,1)} %bitcast.70), calls=%async_computation.5 | async-start | bytes 2621440 | tf_op jit(solution)/shard_map/all_to_all | solution.py:115
  89.9 338.3 %reduce-scatter.8.cloned.1.call-start = ((), (), s32[]{:S(2)}) async-start(), calls=%async_computation.12 | async-start | bytes 3244032 | tf_op jit(solution)/shard_map/reduce_scatter | solution.py:153
  293.7 0.8 copy-start.15
  293.7 10.8 %copy-start.13 = (bf16[320,768]{1,0:T(8,128)(2,1)}, bf16[320,768]{1,0:T(8,128)(2,1)S(1)}, u32[]{:S(2)}) copy-start(bf16[320,768]{1,0:T(8,128)(2,1)S(1)} %get-tuple-element.27) | copy-start | bytes 1474564
  299.4 254.6 %reduce-scatter.6.cloned.1.call-start = ((), (), s32[]{:S(2)}) async-start(), calls=%async_computation.11 | async-start | bytes 3244032 | tf_op jit(solution)/shard_map/reduce_scatter | solution.py:150
  304.5 375.3 %reduce-scatter.4.cloned.1.call-start = ((), (), s32[]{:S(2)}) async-start(), calls=%async_computation.10 | async-start | bytes 3244032 | tf_op jit(solution)/shard_map/reduce_scatter | solution.py:147
  309.4 3.3 copy-start.12
  309.4 3.3 copy-start.14
  315.1 5.0 copy-start.16
  315.1 21.9 %all-to-all-start.6 = ((bf16[8,40,2048]{2,1,0:T(8,128)(2,1)}), bf16[8,40,2048]{2,1,0:T(8,128)(2,1)S(1)}, u32[]{:S(2)}, u32[]{:S(2)}) async-start(bf16[8,40,2048]{2,1,0:T(8,128)(2,1)} %bitcast.16), calls=%async_computation.6 | async-start | bytes 2621440 | tf_op jit(solution)/shard_map/all_to_all | solution.py:130
  337.0 25.4 %all-to-all-start.4 = ((bf16[8,40,2048]{2,1,0:T(8,128)(2,1)}), bf16[8,40,2048]{2,1,0:T(8,128)(2,1)S(1)}, u32[]{:S(2)}, u32[]{:S(2)}) async-start(bf16[8,40,2048]{2,1,0:T(8,128)(2,1)} %bitcast.71), calls=%async_computation.4 | async-start | bytes 2621440 | tf_op jit(solution)/shard_map/all_to_all | solution.py:92
  363.7 2.9 copy-start.4
  366.6 4.9 copy-start.5
  368.8 2.7 copy-start.3
  372.7 308.6 %copy-start.1 = (bf16[1,768,2048]{2,1,0:T(8,128)(2,1)S(1)}, bf16[1,768,2048]{2,1,0:T(8,128)(2,1)}, u32[]{:S(2)}) copy-start(bf16[1,768,2048]{2,1,0:T(8,128)(2,1)} %param.17) | copy-start | bytes 9437188
Sparse Core Ops, SparseCore 0:
  28.3 96.1 all-gather.8
  127.8 79.0 all-gather.10
  210.3 79.6 all-gather.6
  299.5 128.6 reduce-scatter.7
  432.2 121.7 reduce-scatter.5
  558.0 121.7 reduce-scatter.3
where the time goes:
time: 689 us; the launch traced here: 688 us
  waiting for transfers between devices  529 us (77%)
  matrix products  38.3 us (6%)
  starting transfers between devices  32.2 us (5%)
  blocking collectives  29.2 us (4%)
  local copies, waits for them, and re-layouts  21.9 us (3%)
  other arithmetic  21.5 us (3%)
  between operations  16.3 us (2%)
    reduce_scatter x1, waiting for transfers between devices, shards(): lax.psum_scatter(partial_gate.astype(jnp.bfloat16), 'dp', scatter_dimensi...  124 us
    reduce_scatter x1, waiting for transfers between devices, shards(): lax.psum_scatter(partial_up.astype(jnp.bfloat16), 'dp', scatter_dimension...  124 us
    all_gather x1, waiting for transfers between devices, shards(): lax.all_gather(mate_shares[0], 'dp', axis=0, tiled=True)  79.6 us
    all_gather x1, waiting for transfers between devices, shards(): lax.all_gather(mate_shares[2], 'dp', axis=1, tiled=True)  79 us
    reduce_scatter x1, waiting for transfers between devices, shards(): lax.psum_scatter(partial_down.astype(jnp.bfloat16), 'dp', scatter_dimensi...  45 us
    all_gather x1, waiting for transfers between devices, shards(): lax.all_gather(mate_shares[1], 'dp', axis=0, tiled=True)  34.6 us
    all_to_all x2, blocking collectives, shards(): lax.all_to_all(as_sent(outgoing), 'expert', split_axis=0, concat_axis=0,...  29.2 us
    all_to_all x1, waiting for transfers between devices, shards(): lax.all_to_all(expert_out.reshape(groups, capacity, model_width), 'expert...  15.8 us
  transfers between devices with their start and end apart: 11, of which 10 were waited for; matrix products, arithmetic and copies ran while one was open for 10% of the time, Pallas kernels for 0%

commit v1 on v0

--- a/solution.py
+++ b/solution.py
@@ -69,7 +69,9 @@
     )
     mate_shares = tuple((pick_from(block_piece, my_mate) for block_piece in incoming))
     gate_mat, up_mat, down_mat = (
-        lax.all_gather(mate_shares[0], "dp", axis=0, tiled=True),
+        jnp.concatenate(
+            lax.all_to_all(jnp.stack([mate_shares[0]] * lax.axis_size("dp")), "dp", 0, 0), axis=0
+        ),
         lax.all_gather(mate_shares[1], "dp", axis=0, tiled=True),
         lax.all_gather(mate_shares[2], "dp", axis=1, tiled=True),
     )

time: 689 us -> 626 us (0.909)
  waiting for transfers between devices: 529 us -> 468 us
  blocking collectives: 29.2 us -> 0 us
  starting transfers between devices: 32.2 us -> 55.7 us
    all_gather x1 -> x0, waiting for transfers between devices: 79.6 us -> none  [shards(): lax.all_gather(mate_shares[0], 'dp', axis=0, tiled=True)]
    all_to_all x0 -> x1, waiting for transfers between devices: none -> 72.3 us  [shards(): lax.all_to_all(jnp.stack([mate_shares[0]] * lax.axis_size('dp')), 'dp', 0...]
    all_gather x1, waiting for transfers between devices: 79 us -> 26.6 us  [shards(): lax.all_gather(mate_shares[2], 'dp', axis=1, tiled=True)]
    all_gather x1, waiting for transfers between devices: 34.6 us -> 0.02 us  [shards(): lax.all_gather(mate_shares[1], 'dp', axis=0, tiled=True)]
    all_to_all x2 -> x0, blocking collectives: 29.2 us -> none  [shards(): lax.all_to_all(as_sent(outgoing), 'expert', split_axis=0, concat_axis=0,...]
    all_to_all x1 -> x3, waiting for transfers between devices: 7.28 us -> 20.6 us  [shards(): lax.all_to_all(as_sent(outgoing), 'expert', split_axis=0, concat_axis=0,...]
    all_to_all x1 -> x3, starting transfers between devices: 6.32 us -> 18.4 us  [shards(): lax.all_to_all(as_sent(outgoing), 'expert', split_axis=0, concat_axis=0,...]
    all_to_all x0 -> x1, starting transfers between devices: none -> 12 us  [shards(): lax.all_to_all(jnp.stack([mate_shares[0]] * lax.axis_size('dp')), 'dp', 0...]
  transfers between devices with their start and end apart: 11 -> 13, of which waited for: 10 -> 12; matrix products, arithmetic and copies ran while one was open for 10% -> 11% of each run, Pallas kernels for 0% -> 0%
where the time goes in v1:
time: 626 us; the launch traced here: 625 us
  waiting for transfers between devices  468 us (75%)
  starting transfers between devices  55.7 us (9%)
  matrix products  37.7 us (6%)
  local copies, waits for them, and re-layouts  25.2 us (4%)
  other arithmetic  22.4 us (4%)
  between operations  15.9 us (3%)
    reduce_scatter x1, waiting for transfers between devices, shards(): lax.psum_scatter(partial_gate.astype(jnp.bfloat16), 'dp', scatter_dimensi...  124 us
    reduce_scatter x1, waiting for transfers between devices, shards(): lax.psum_scatter(partial_up.astype(jnp.bfloat16), 'dp', scatter_dimension...  124 us
    all_to_all x1, waiting for transfers between devices, shards(): lax.all_to_all(jnp.stack([mate_shares[0]] * lax.axis_size('dp')), 'dp', 0...  72.3 us
    reduce_scatter x1, waiting for transfers between devices, shards(): lax.psum_scatter(partial_down.astype(jnp.bfloat16), 'dp', scatter_dimensi...  45.9 us
    all_gather x1, waiting for transfers between devices, shards(): lax.all_gather(mate_shares[2], 'dp', axis=1, tiled=True)  26.6 us
    all_to_all x3, waiting for transfers between devices, shards(): lax.all_to_all(as_sent(outgoing), 'expert', split_axis=0, concat_axis=0,...  20.6 us
    all_to_all x3, starting transfers between devices, shards(): lax.all_to_all(as_sent(outgoing), 'expert', split_axis=0, concat_axis=0,...  18.4 us
    all_to_all x1, waiting for transfers between devices, shards(): lax.all_to_all(expert_out.reshape(groups, capacity, model_width), 'expert...  14.7 us
  transfers between devices with their start and end apart: 13, of which 12 were waited for; matrix products, arithmetic and copies ran while one was open for 11% of the time, Pallas kernels for 0%

profile of v1, /device:TPU:4, one launch (start us, length us, event | category | flops | bytes accessed | tf_op | source)
XLA Modules:
  0.0 624.6 jit_solution(2728377487406714974)
XLA Ops:
  7.2 0.8 broadcast_compare_fusion
  8.0 1.1 dynamic-slice_bitcast_fusion
  9.1 1.3 broadcast_select_fusion.3
  10.4 6.5 %all-to-all-start.3 = ((bf16[8,64,768]{2,1,0:T(8,128)(2,1)}), bf16[8,64,768]{2,1,0:T(8,128)(2,1)}, u32[]{:S(2)}, u32[]{:S(2)}) async-start(bf16[8,64,768]{2,1,0:T(8,128)(2,1)} %get-tuple-element.33), calls=%async_computation.3 | async-start | bytes 1572864 | tf_op jit(solution)/shard_map/all_to_all | solution.py:67
  16.9 0.6 dynamic_slice.27
  19.4 7.3 %all-to-all-done.3 = bf16[8,64,768]{2,1,0:T(8,128)(2,1)} async-done(((bf16[8,64,768]{2,1,0:T(8,128)(2,1)}), bf16[8,64,768]{2,1,0:T(8,128)(2,1)}, u32[]{:S(2)}, u32[]{:S(2)}) %all-to-all-start.3) | async-done | bytes 786464 | tf_op jit(solution)/shard_map/all_to_all | solution.py:67
  26.7 1.5 constant_dynamic-slice_fusion.2
  28.3 6.3 %all-to-all-start.1 = ((bf16[8,64,768]{2,1,0:T(8,128)(2,1)}), bf16[8,64,768]{2,1,0:T(8,128)(2,1)}, u32[]{:S(2)}, u32[]{:S(2)}) async-start(bf16[8,64,768]{2,1,0:T(8,128)(2,1)} %get-tuple-element.32), calls=%async_computation.1 | async-start | bytes 1572864 | tf_op jit(solution)/shard_map/all_to_all | solution.py:67
  34.7 0.1 eq.57
  34.9 0.6 reduce-window.6
  35.8 1.0 broadcast_select_fusion.1
  36.8 6.8 %all-to-all-done.1 = bf16[8,64,768]{2,1,0:T(8,128)(2,1)} async-done(((bf16[8,64,768]{2,1,0:T(8,128)(2,1)}), bf16[8,64,768]{2,1,0:T(8,128)(2,1)}, u32[]{:S(2)}, u32[]{:S(2)}) %all-to-all-start.1) | async-done | bytes 786464 | tf_op jit(solution)/shard_map/all_to_all | solution.py:67
  43.6 5.6 all-to-all-start.4
  49.3 0.2 slice_reduce_fusion
  49.5 0.6 broadcast_in_dim.123
  50.2 0.4 reshape.96
  50.7 1.6 convolution_convert_fusion.4
  52.3 6.5 %all-to-all-done.4 = bf16[8,768,64]{1,2,0:T(8,128)(2,1)S(1)} async-done(((bf16[8,768,64]{1,2,0:T(8,128)(2,1)}), bf16[8,768,64]{1,2,0:T(8,128)(2,1)S(1)}, u32[]{:S(2)}, u32[]{:S(2)}) %all-to-all-start.4) | async-done | bytes 786464 | tf_op jit(solution)/shard_map/all_to_all | solution.py:67
  58.8 5.7 all-to-all-start
  64.5 0.9 dynamic-slice_bitcast_fusion.1
  65.4 14.3 %all-to-all-done = bf16[8,40,2048]{2,1,0:T(8,128)(2,1)S(1)} async-done(((bf16[8,40,2048]{2,1,0:T(8,128)(2,1)}), bf16[8,40,2048]{2,1,0:T(8,128)(2,1)S(1)}, u32[]{:S(2)}, u32[]{:S(2)}) %all-to-all-start) | async-done | bytes 1310752 | tf_op jit(solution)/shard_map/all_to_all | solution.py:82
  79.7 2.2 stack.2
  81.9 12.0 %all-to-all-start.2 = ((bf16[32,64,768]{2,1,0:T(8,128)(2,1)}), bf16[32,64,768]{2,1,0:T(8,128)(2,1)}, u32[]{:S(2)}, u32[]{:S(2)}) async-start(bf16[32,64,768]{2,1,0:T(8,128)(2,1)} %stack.2), calls=%async_computation.2 | async-start | bytes 6291456 | tf_op jit(solution)/shard_map/all_to_all | solution.py:73
  93.9 0.7 constant_dynamic-slice_fusion
  94.6 2.4 mul.83
  97.1 2.7 mul.84
  99.9 0.1 mul.81
  100.1 1.6 convolution_convert_fusion.3
  101.7 72.3 %all-to-all-done.2 = bf16[32,64,768]{2,1,0:T(8,128)(2,1)} async-done(((bf16[32,64,768]{2,1,0:T(8,128)(2,1)}), bf16[32,64,768]{2,1,0:T(8,128)(2,1)}, u32[]{:S(2)}, u32[]{:S(2)}) %all-to-all-start.2) | async-done | bytes 3145760 | tf_op jit(solution)/shard_map/all_to_all | solution.py:73
  174.0 7.0 %all-to-all-start.6 = ((bf16[8,40,2048]{2,1,0:T(8,128)(2,1)}), bf16[8,40,2048]{2,1,0:T(8,128)(2,1)}, u32[]{:S(2)}, u32[]{:S(2)}) async-start(bf16[8,40,2048]{2,1,0:T(8,128)(2,1)} %bitcast.70), calls=%async_computation.6 | async-start | bytes 2621440 | tf_op jit(solution)/shard_map/all_to_all | solution.py:117
  181.0 3.9 fusion.23
  184.9 4.0 fusion.6
  188.9 11.8 %all-to-all-done.6 = bf16[8,40,2048]{2,1,0:T(8,128)(2,1)} async-done(((bf16[8,40,2048]{2,1,0:T(8,128)(2,1)}), bf16[8,40,2048]{2,1,0:T(8,128)(2,1)}, u32[]{:S(2)}, u32[]{:S(2)}) %all-to-all-start.6) | async-done | bytes 1310752 | tf_op jit(solution)/shard_map/all_to_all | solution.py:117
  200.7 26.6 %all-gather.7.cloned.1.call-done = bf16[1,768,2048]{1,2,0:T(8,128)(2,1)} async-done(((bf16[1,768,64]{1,2,0:T(8,128)(2,1)}), bf16[1,768,2048]{1,2,0:T(8,128)(2,1)}) %all-gather.7.cloned.1.call-update) | async-done | bytes 3145744 | tf_op jit(solution)/shard_map/all_gather | solution.py:76
  227.3 4.7 multiply_convert_fusion.2
  232.0 0.8 copy-done.17
  232.8 4.8 convolution_convert_fusion
  237.7 0.2 reduce-scatter.6.cloned.1.call-start
  237.9 0.8 copy-done.15
  238.7 3.5 convolution_convert_fusion.1
  242.3 3.6 convolution_convert_fusion.2
  245.9 3.5 fusion.24
  249.4 2.3 fusion.11
  251.7 5.2 all-to-all-start.7
  256.9 4.2 fusion.14
  261.1 12.7 %all-to-all-done.7 = bf16[8,40,2048]{2,1,0:T(8,128)(2,1)S(1)} async-done(((bf16[8,40,2048]{2,1,0:T(8,128)(2,1)}), bf16[8,40,2048]{2,1,0:T(8,128)(2,1)S(1)}, u32[]{:S(2)}, u32[]{:S(2)}) %all-to-all-start.7) | async-done | bytes 1310752 | tf_op jit(solution)/shard_map/all_to_all | solution.py:132
  273.8 7.2 %all-to-all-start.5 = ((bf16[8,40,2048]{2,1,0:T(8,128)(2,1)}), bf16[8,40,2048]{2,1,0:T(8,128)(2,1)S(1)}, u32[]{:S(2)}, u32[]{:S(2)}) async-start(bf16[8,40,2048]{2,1,0:T(8,128)(2,1)} %bitcast.75), calls=%async_computation.5 | async-start | bytes 2621440 | tf_op jit(solution)/shard_map/all_to_all | solution.py:94
  281.0 2.3 gather_fusion.1
  283.4 14.7 %all-to-all-done.5 = bf16[8,40,2048]{2,1,0:T(8,128)(2,1)S(1)} async-done(((bf16[8,40,2048]{2,1,0:T(8,128)(2,1)}), bf16[8,40,2048]{2,1,0:T(8,128)(2,1)S(1)}, u32[]{:S(2)}, u32[]{:S(2)}) %all-to-all-start.5) | async-done | bytes 1310752 | tf_op jit(solution)/shard_map/all_to_all | solution.py:94
  298.1 1.4 gather_fusion
  299.4 2.9 broadcast_select_fusion
  302.3 2.2 reshape.102
  304.5 2.7 reshape.107
  307.2 0.4 multiply_reduce_fusion
  307.7 0.1 reduce_sum.52
  307.8 0.6 copy.27
  308.4 4.7 reduce.1
  313.2 5.6 multiply_reduce_fusion.1
  318.8 45.9 %reduce-scatter.8.cloned.1.call-done = bf16[768,64]{0,1:T(8,128)(2,1)} async-done(((bf16[768,2048]{0,1:T(8,128)(2,1)}), bf16[768,64]{0,1:T(8,128)(2,1)}) %reduce-scatter.8.cloned.1.call-update) | async-done | bytes 98320 | tf_op jit(solution)/shard_map/reduce_scatter | solution.py:155
  364.7 1.6 bitcast_convert_fusion
  366.2 124.3 %reduce-scatter.6.cloned.1.call-done = bf16[64,768]{1,0:T(8,128)(2,1)} async-done(((bf16[2048,768]{1,0:T(8,128)(2,1)}), bf16[64,768]{1,0:T(8,128)(2,1)}) %reduce-scatter.6.cloned.1.call-update) | async-done | bytes 98320 | tf_op jit(solution)/shard_map/reduce_scatter | solution.py:152
  490.5 1.6 bitcast_convert_fusion.1
  492.1 124.3 %reduce-scatter.4.cloned.1.call-done = bf16[64,768]{1,0:T(8,128)(2,1)} async-done(((bf16[2048,768]{1,0:T(8,128)(2,1)}), bf16[64,768]{1,0:T(8,128)(2,1)}) %reduce-scatter.4.cloned.1.call-update) | async-done | bytes 98320 | tf_op jit(solution)/shard_map/reduce_scatter | solution.py:149
  616.5 1.6 bitcast_convert_fusion.2
  (58 shorter events, 1.0 us)
Async XLA Ops:
  7.2 28.3 %copy-start = (bf16[1,768,2048]{2,1,0:T(8,128)(2,1)S(1)}, bf16[1,768,2048]{2,1,0:T(8,128)(2,1)}, u32[]{:S(2)}) copy-start(bf16[1,768,2048]{2,1,0:T(8,128)(2,1)} %param.17) | copy-start | bytes 9437188
  7.2 9.7 %copy-start.12 = (s32[8]{0:T(128)S(1)}, s32[8]{0:T(128)}, u32[]{:S(2)}) copy-start(s32[8]{0:T(128)} %param.14) | copy-start | bytes 100
  10.4 24.1 %copy-start.10 = (s32[128,2]{0,1:T(2,128)S(1)}, s32[128,2]{0,1:T(2,128)}, u32[]{:S(2)}) copy-start(s32[128,2]{0,1:T(2,128)} %param.12) | copy-start | bytes 3076
  10.4 16.3 %all-to-all-start.3 = ((bf16[8,64,768]{2,1,0:T(8,128)(2,1)}), bf16[8,64,768]{2,1,0:T(8,128)(2,1)}, u32[]{:S(2)}, u32[]{:S(2)}) async-start(bf16[8,64,768]{2,1,0:T(8,128)(2,1)} %get-tuple-element.33), calls=%async_computation.3 | async-start | bytes 1572864 | tf_op jit(solution)/shard_map/all_to_all | solution.py:67
  16.9 168.0 %all-gather.5.cloned.1.call-start = ((), (), s32[]{:S(2)}) async-start(), calls=%async_computation.14 | async-start | bytes 3244032 | tf_op jit(solution)/shard_map/all_gather | solution.py:75
  28.3 15.3 %all-to-all-start.1 = ((bf16[8,64,768]{2,1,0:T(8,128)(2,1)}), bf16[8,64,768]{2,1,0:T(8,128)(2,1)}, u32[]{:S(2)}, u32[]{:S(2)}) async-start(bf16[8,64,768]{2,1,0:T(8,128)(2,1)} %get-tuple-element.32), calls=%async_computation.1 | async-start | bytes 1572864 | tf_op jit(solution)/shard_map/all_to_all | solution.py:67
  35.6 13.9 %copy-start.8 = (bf16[128,2048]{1,0:T(8,128)(2,1)S(1)}, bf16[128,2048]{1,0:T(8,128)(2,1)}, u32[]{:S(2)}) copy-start(bf16[128,2048]{1,0:T(8,128)(2,1)} %param.10) | copy-start | bytes 1572868
  43.6 15.2 %all-to-all-start.4 = ((bf16[8,768,64]{1,2,0:T(8,128)(2,1)}), bf16[8,768,64]{1,2,0:T(8,128)(2,1)S(1)}, u32[]{:S(2)}, u32[]{:S(2)}) async-start(bf16[8,768,64]{1,2,0:T(8,128)(2,1)} %broadcast_select_fusion.1), calls=%async_computation.4 | async-start | bytes 1572864 | tf_op jit(solution)/shard_map/all_to_all | solution.py:67
  58.8 20.9 %all-to-all-start = ((bf16[8,40,2048]{2,1,0:T(8,128)(2,1)}), bf16[8,40,2048]{2,1,0:T(8,128)(2,1)S(1)}, u32[]{:S(2)}, u32[]{:S(2)}) async-start(bf16[8,40,2048]{2,1,0:T(8,128)(2,1)} %bitcast.3), calls=%async_computation | async-start | bytes 2621440 | tf_op jit(solution)/shard_map/all_to_all | solution.py:82
  79.7 2.2 copy-start.6
  81.9 12.7 %copy-start.9 = (bf16[128,2048]{1,0:T(8,128)(2,1)S(1)}, bf16[128,2048]{1,0:T(8,128)(2,1)}, u32[]{:S(2)}) copy-start(bf16[128,2048]{1,0:T(8,128)(2,1)} %param.11) | copy-start | bytes 1572868
  81.9 92.1 %all-to-all-start.2 = ((bf16[32,64,768]{2,1,0:T(8,128)(2,1)}), bf16[32,64,768]{2,1,0:T(8,128)(2,1)}, u32[]{:S(2)}, u32[]{:S(2)}) async-start(bf16[32,64,768]{2,1,0:T(8,128)(2,1)} %stack.2), calls=%async_computation.2 | async-start | bytes 6291456 | tf_op jit(solution)/shard_map/all_to_all | solution.py:73
  93.9 133.4 %all-gather.7.cloned.1.call-start = ((), (), s32[]{:S(2)}) async-start(), calls=%async_computation.15 | async-start | bytes 3244032 | tf_op jit(solution)/shard_map/all_gather | solution.py:76
  97.1 2.7 copy-start.11
  99.8 74.2 %copy-start.2 = (f32[256,2048]{1,0:T(8,128)}, f32[256,2048]{1,0:T(8,128)S(1)}, u32[]{:S(2)}) copy-start(f32[256,2048]{1,0:T(8,128)S(1)} %mul.84) | copy-start | bytes 6291460
  174.0 26.7 %all-to-all-start.6 = ((bf16[8,40,2048]{2,1,0:T(8,128)(2,1)}), bf16[8,40,2048]{2,1,0:T(8,128)(2,1)}, u32[]{:S(2)}, u32[]{:S(2)}) async-start(bf16[8,40,2048]{2,1,0:T(8,128)(2,1)} %bitcast.70), calls=%async_computation.6 | async-start | bytes 2621440 | tf_op jit(solution)/shard_map/all_to_all | solution.py:117
  181.0 183.7 %reduce-scatter.8.cloned.1.call-start = ((), (), s32[]{:S(2)}) async-start(), calls=%async_computation.13 | async-start | bytes 3244032 | tf_op jit(solution)/shard_map/reduce_scatter | solution.py:155
  181.0 3.9 copy-start.7
  232.0 0.8 copy-start.17
  232.0 10.2 %copy-start.14 = (bf16[320,768]{1,0:T(8,128)(2,1)}, bf16[320,768]{1,0:T(8,128)(2,1)S(1)}, u32[]{:S(2)}) copy-start(bf16[320,768]{1,0:T(8,128)(2,1)S(1)} %get-tuple-element.28) | copy-start | bytes 1474564
  237.7 1.0 copy-start.15
  237.7 252.9 %reduce-scatter.6.cloned.1.call-start = ((), (), s32[]{:S(2)}) async-start(), calls=%async_computation.12 | async-start | bytes 3244032 | tf_op jit(solution)/shard_map/reduce_scatter | solution.py:152
  242.2 374.2 %reduce-scatter.4.cloned.1.call-start = ((), (), s32[]{:S(2)}) async-start(), calls=%async_computation.11 | async-start | bytes 3244032 | tf_op jit(solution)/shard_map/reduce_scatter | solution.py:149
  245.9 3.5 copy-start.13
  245.9 3.5 copy-start.16
  251.7 5.2 copy-start.18
  251.7 22.1 %all-to-all-start.7 = ((bf16[8,40,2048]{2,1,0:T(8,128)(2,1)}), bf16[8,40,2048]{2,1,0:T(8,128)(2,1)S(1)}, u32[]{:S(2)}, u32[]{:S(2)}) async-start(bf16[8,40,2048]{2,1,0:T(8,128)(2,1)} %bitcast.17), calls=%async_computation.7 | async-start | bytes 2621440 | tf_op jit(solution)/shard_map/all_to_all | solution.py:132
  273.8 24.3 %all-to-all-start.5 = ((bf16[8,40,2048]{2,1,0:T(8,128)(2,1)}), bf16[8,40,2048]{2,1,0:T(8,128)(2,1)S(1)}, u32[]{:S(2)}, u32[]{:S(2)}) async-start(bf16[8,40,2048]{2,1,0:T(8,128)(2,1)} %bitcast.75), calls=%async_computation.5 | async-start | bytes 2621440 | tf_op jit(solution)/shard_map/all_to_all | solution.py:94
  299.4 2.9 copy-start.4
  302.3 4.9 copy-start.5
  304.5 2.7 copy-start.3
  308.4 309.6 %copy-start.1 = (bf16[1,768,2048]{2,1,0:T(8,128)(2,1)S(1)}, bf16[1,768,2048]{2,1,0:T(8,128)(2,1)}, u32[]{:S(2)}) copy-start(bf16[1,768,2048]{2,1,0:T(8,128)(2,1)} %param.17) | copy-start | bytes 9437188
Sparse Core Ops, SparseCore 0:
  28.4 92.7 all-gather.4
  124.5 102.7 all-gather.6
  237.8 126.8 reduce-scatter.7
  368.7 121.8 reduce-scatter.5
  494.6 121.8 reduce-scatter.3
